TPU v7x, 32 devices: a whole 2x2x4 slice. The times are simulated.
32 devices in a mesh: row: 8 (over z, y), col: 4 (over x, core).
Axes of the slice: x: 2, y: 2, z: 4, core: 2. Of those that a mesh axis runs over, the one named last changes fastest.
Arguments:
- weights: bfloat16 [2, 8192, 8192], P(None, 'row', 'col'), may hold values from -0.0625 to 0.0625
- preact: float32 [2, 2, 8192], P(None, None, 'row'), may hold values from -2.5 to 2.5
- panel: bfloat16 [2, 64, 8192], P(None, None, 'col'), may hold values from -6 to 6
Outputs:
- basis_out: float32 [2, 64, 8192], P(None, None, 'col')
All inputs are finite; a program needn't handle non-finite values.
Results may differ from a plain program's by a relative error of at most 0.035.
Values may be sent and summed in bfloat16 or wider, within the bound.
A program may use at most 64 MiB of HBM per device.

v0:
```python
from functools import partial
import jax
import jax.numpy as jnp
from jax import lax
from jax.sharding import PartitionSpec as P

WIDTH = 8192
ITERS = 2


def on_device(weights, preact, panel):
    slopes = 1.0 - jnp.tanh(preact) ** 2
    layers = weights.shape[0]
    current = panel
    basis_out = panel.astype(jnp.float32)
    for iteration in range(ITERS):
        cotangent = None
        for layer_at in range(layers):
            partial_out = jnp.einsum(
                "bki,oi->bko", current, weights[layer_at], preferred_element_type=jnp.float32
            )
            summed = lax.psum_scatter(
                partial_out.astype(jnp.bfloat16), "col", scatter_dimension=1, tiled=True
            ).astype(jnp.float32)
            scaled = (slopes[:, layer_at, None, :] * summed).astype(jnp.bfloat16)
            if layer_at + 1 < layers:
                spread = lax.all_gather(scaled, "row", axis=2, tiled=True)
                current = lax.all_to_all(spread, "col", split_axis=2, concat_axis=1, tiled=True)
            else:
                cotangent = lax.all_gather(scaled, "col", axis=1, tiled=True)
        image_panel = None
        for layer_at in reversed(range(layers)):
            weighted = (slopes[:, layer_at, None, :] * cotangent).astype(jnp.bfloat16)
            partial_in = jnp.einsum(
                "bko,oi->bki", weighted, weights[layer_at], preferred_element_type=jnp.float32
            )
            if layer_at == 0:
                pieces = lax.psum_scatter(
                    partial_in.astype(jnp.bfloat16), "row", scatter_dimension=2, tiled=True
                )
                image_panel = lax.all_gather(pieces, "row", axis=2, tiled=True)
            else:
                pieces = lax.psum_scatter(
                    partial_in.astype(jnp.bfloat16), "row", scatter_dimension=1, tiled=True
                )
                spread = lax.all_gather(pieces, "col", axis=2, tiled=True)
                cotangent = lax.all_to_all(spread, "row", split_axis=2, concat_axis=1, tiled=True)
        local_gram = jnp.einsum(
            "bkw,bjw->bkj", image_panel, image_panel, preferred_element_type=jnp.float32
        )
        gram_sum = lax.psum(local_gram.astype(jnp.bfloat16), "col").astype(jnp.float32)
        factor = jnp.linalg.cholesky(gram_sum / WIDTH)
        basis_out = jax.vmap(partial(jax.scipy.linalg.solve_triangular, lower=True))(
            factor, image_panel.astype(jnp.float32)
        )
        current = basis_out.astype(jnp.bfloat16)
    return basis_out


def solution(mesh):
    return jax.shard_map(
        on_device,
        mesh=mesh,
        in_specs=(P(None, "row", "col"), P(None, None, "row"), P(None, None, "col")),
        out_specs=P(None, None, "col"),
        check_vma=False,
    )
```

profile of v0, /device:TPU:0, one launch (start us, length us, event | category | flops | bytes accessed | tf_op | source)
XLA Modules:
  0.0 776.8 jit_solution(17862595918340202358)
XLA Ops:
  12.1 22.8 %reduce-scatter.13.cloned.1.call-done = bf16[2,16,1024]{2,1,0:T(8,128)(2,1)} async-done(((bf16[2,64,1024]{2,1,0:T(8,128)(2,1)}), bf16[2,16,1024]{2,1,0:T(8,128)(2,1)}) %reduce-scatter.13.cloned.1.call-update) | async-done | bytes 65552 | tf_op jit(solution)/shard_map/reduce_scatter | solution.py:22
  35.8 31.6 %all_gather.24 = bf16[2,16,8192]{2,1,0:T(8,128)(2,1)S(1)} all-gather(bf16[2,16,1024]{2,1,0:T(8,128)(2,1)S(1)} %multiply_convert_fusion.7), channel_id=1, replica_groups=mesh['row'=8,'col'=4] {'row'}, dimensions={2}, use_global_device_ids=true | all-gather | bytes 589824 | tf_op jit(solution)/shard_map/all_gather | solution.py:27
  67.4 6.7 copy.47
  79.9 11.2 %all_to_all.54 = bf16[4,2,32768]{2,1,0:T(2,128)(2,1)S(1)} all-to-all(bf16[4,2,32768]{2,1,0:T(2,128)(2,1)S(1)} %reshape.23), channel_id=1, replica_groups=mesh['row'=8,'col'=4] {'col'}, dimensions={0} | all-to-all | bytes 1048576 | tf_op jit(solution)/shard_map/all_to_all | solution.py:28
  95.2 9.7 %copy.67 = bf16[2,16,4,2048]{3,2,1,0:T(4,128)(2,1)S(1)} copy(bf16[2,16,4,2048]{1,0,3,2:T(2,128)(2,1)} %bitcast.105) | data formatting | bytes 1048576 | tf_op jit(solution)/shard_map/all_to_all | solution.py:28
  109.7 20.0 %reduce-scatter.15.cloned.1.call-done = bf16[2,16,1024]{2,1,0:T(8,128)(2,1)} async-done(((bf16[2,64,1024]{2,1,0:T(8,128)(2,1)}), bf16[2,16,1024]{2,1,0:T(8,128)(2,1)}) %reduce-scatter.15.cloned.1.call-update) | async-done | bytes 65552 | tf_op jit(solution)/shard_map/reduce_scatter | solution.py:22
  140.9 63.2 %reduce-scatter.25.cloned.1.call-done = bf16[8,4096]{1,0:T(8,128)(2,1)} async-done(((bf16[64,4096]{1,0:T(8,128)(2,1)}), bf16[8,4096]{1,0:T(8,128)(2,1)}) %reduce-scatter.25.cloned.1.call-update) | async-done | bytes 65552
  210.7 6.7 copy.50
  227.8 9.0 %all-to-all-done.1 = bf16[8,2,8192]{2,1,0:T(2,128)(2,1)S(1)} async-done(((bf16[8,2,8192]{2,1,0:T(2,128)(2,1)}), bf16[8,2,8192]{2,1,0:T(2,128)(2,1)S(1)}, u32[]{:S(2)}, u32[]{:S(2)}) %all-to-all-start.1) | async-done | bytes 262176 | tf_op jit(solution)/shard_map/all_to_all | solution.py:47
  242.8 7.5 fusion.2
  250.3 8.9 %copy.51 = bf16[2,8,8,1024]{3,2,1,0:T(8,128)(2,1)S(1)} copy(bf16[2,8,8,1024]{2,0,3,1:T(2,128)(2,1)} %fusion.2) | data formatting | bytes 524288 | tf_op jit(solution)/shard_map/convert_element_type | solution.py:33
  263.0 62.1 %reduce-scatter.17.cloned.1.call-done = bf16[2,64,256]{2,1,0:T(8,128)(2,1)} async-done(((bf16[2,64,2048]{2,1,0:T(8,128)(2,1)}), bf16[2,64,256]{2,1,0:T(8,128)(2,1)}) %reduce-scatter.17.cloned.1.call-update) | async-done | bytes 65552 | tf_op jit(solution)/shard_map/reduce_scatter | solution.py:38
  325.1 31.8 %all_gather.27 = bf16[2,64,2048]{2,1,0:T(8,128)(2,1)S(1)} all-gather(bf16[2,64,256]{2,1,0:T(8,128)(2,1)} %reduce-scatter.17.cloned.1.call-done), channel_id=1, replica_groups=mesh['row'=8,'col'=4] {'row'}, dimensions={2}, use_global_device_ids=true | all-gather | bytes 589824 | tf_op jit(solution)/shard_map/all_gather | solution.py:41
  357.2 10.3 %psum.14 = bf16[2,64,64]{1,2,0:T(8,128)(2,1)S(1)} all-reduce(bf16[2,64,64]{1,2,0:T(8,128)(2,1)S(1)} %convolution_convert_fusion.2), channel_id=1, replica_groups=mesh['row'=8,'col'=4] {'col'}, use_global_device_ids=true, to_apply=%region_4.0 | all-reduce | flops 8192 | bytes 32768 | tf_op jit(solution)/shard_map/psum | solution.py:51
  367.6 11.7 %custom-call.8 = f32[2,64,64]{2,1,0:T(8,128)S(1)} custom-call(f32[2,64,64]{2,1,0:T(8,128)S(1)} %fusion.62), custom_call_target="Cholesky" | custom-call | tf_op jit(solution)/shard_map/jit(cholesky)/cholesky | solution.py:52
  379.6 9.8 %custom-call.9 = f32[2,1,64,64]{2,3,1,0:T(8,128)S(1)} custom-call(f32[2,1,64,64]{3,2,1,0:T(8,128)S(1)} %select_bitcast_fusion.1), custom_call_target="InvertDiagBlocksLowerTriangular" | custom-call | tf_op jit(solution)/shard_map/vmap(jit(_solve_triangular))/triangular_solve | solution.py:53
  395.0 19.1 %reduce-scatter.19.cloned.1.call-done = bf16[2,16,1024]{2,1,0:T(8,128)(2,1)} async-done(((bf16[2,64,1024]{2,1,0:T(8,128)(2,1)}), bf16[2,16,1024]{2,1,0:T(8,128)(2,1)}) %reduce-scatter.19.cloned.1.call-update) | async-done | bytes 65552 | tf_op jit(solution)/shard_map/reduce_scatter | solution.py:22
  414.9 31.5 %all_gather.28 = bf16[2,16,8192]{2,1,0:T(8,128)(2,1)S(1)} all-gather(bf16[2,16,1024]{2,1,0:T(8,128)(2,1)S(1)} %multiply_convert_fusion.5), channel_id=1, replica_groups=mesh['row'=8,'col'=4] {'row'}, dimensions={2}, use_global_device_ids=true | all-gather | bytes 589824 | tf_op jit(solution)/shard_map/all_gather | solution.py:27
  446.4 6.7 copy.55
  458.8 11.2 %all_to_all.55 = bf16[4,2,32768]{2,1,0:T(2,128)(2,1)S(1)} all-to-all(bf16[4,2,32768]{2,1,0:T(2,128)(2,1)S(1)} %reshape.27), channel_id=1, replica_groups=mesh['row'=8,'col'=4] {'col'}, dimensions={0} | all-to-all | bytes 1048576 | tf_op jit(solution)/shard_map/all_to_all | solution.py:28
  474.2 9.7 %copy.68 = bf16[2,16,4,2048]{3,2,1,0:T(4,128)(2,1)S(1)} copy(bf16[2,16,4,2048]{1,0,3,2:T(2,128)(2,1)} %bitcast.107) | data formatting | bytes 1048576 | tf_op jit(solution)/shard_map/all_to_all | solution.py:28
  488.7 20.2 %reduce-scatter.21.cloned.1.call-done = bf16[2,16,1024]{2,1,0:T(8,128)(2,1)} async-done(((bf16[2,64,1024]{2,1,0:T(8,128)(2,1)}), bf16[2,16,1024]{2,1,0:T(8,128)(2,1)}) %reduce-scatter.21.cloned.1.call-update) | async-done | bytes 65552 | tf_op jit(solution)/shard_map/reduce_scatter | solution.py:22
  520.0 63.2 %reduce-scatter.27.cloned.1.call-done = bf16[8,4096]{1,0:T(8,128)(2,1)} async-done(((bf16[64,4096]{1,0:T(8,128)(2,1)}), bf16[8,4096]{1,0:T(8,128)(2,1)}) %reduce-scatter.27.cloned.1.call-update) | async-done | bytes 65552
  589.9 6.7 copy.58
  602.3 12.8 %all_to_all.56 = bf16[8,2,8192]{2,1,0:T(2,128)(2,1)S(1)} all-to-all(bf16[8,2,8192]{2,1,0:T(2,128)(2,1)S(1)} %reshape.29), channel_id=1, replica_groups=mesh['row'=8,'col'=4] {'row'}, dimensions={0} | all-to-all | bytes 524288 | tf_op jit(solution)/shard_map/all_to_all | solution.py:47
  621.1 7.5 fusion.3
  628.6 8.9 %copy.59 = bf16[2,8,8,1024]{3,2,1,0:T(8,128)(2,1)S(1)} copy(bf16[2,8,8,1024]{2,0,3,1:T(2,128)(2,1)} %fusion.3) | data formatting | bytes 524288 | tf_op jit(solution)/shard_map/convert_element_type | solution.py:33
  641.3 62.3 %reduce-scatter.23.cloned.1.call-done = bf16[2,64,256]{2,1,0:T(8,128)(2,1)} async-done(((bf16[2,64,2048]{2,1,0:T(8,128)(2,1)}), bf16[2,64,256]{2,1,0:T(8,128)(2,1)}) %reduce-scatter.23.cloned.1.call-update) | async-done | bytes 65552 | tf_op jit(solution)/shard_map/reduce_scatter | solution.py:38
  703.6 31.6 %all_gather.31 = bf16[2,64,2048]{2,1,0:T(8,128)(2,1)S(1)} all-gather(bf16[2,64,256]{2,1,0:T(8,128)(2,1)} %reduce-scatter.23.cloned.1.call-done), channel_id=1, replica_groups=mesh['row'=8,'col'=4] {'row'}, dimensions={2}, use_global_device_ids=true | all-gather | bytes 589824 | tf_op jit(solution)/shard_map/all_gather | solution.py:41
  735.5 10.5 %psum.15 = bf16[2,64,64]{1,2,0:T(8,128)(2,1)S(1)} all-reduce(bf16[2,64,64]{1,2,0:T(8,128)(2,1)S(1)} %convolution_convert_fusion.1), channel_id=1, replica_groups=mesh['row'=8,'col'=4] {'col'}, use_global_device_ids=true, to_apply=%region_11.14 | all-reduce | flops 8192 | bytes 32768 | tf_op jit(solution)/shard_map/psum | solution.py:51
  746.2 11.7 %custom-call.10 = f32[2,64,64]{2,1,0:T(8,128)S(1)} custom-call(f32[2,64,64]{2,1,0:T(8,128)S(1)} %fusion.60), custom_call_target="Cholesky" | custom-call | tf_op jit(solution)/shard_map/jit(cholesky)/cholesky | solution.py:52
  758.1 9.8 %custom-call.11 = f32[2,1,64,64]{2,3,1,0:T(8,128)S(1)} custom-call(f32[2,1,64,64]{3,2,1,0:T(8,128)S(1)} %select_bitcast_fusion), custom_call_target="InvertDiagBlocksLowerTriangular" | custom-call | tf_op jit(solution)/shard_map/vmap(jit(_solve_triangular))/triangular_solve | solution.py:53
  (80 shorter events, 116.5 us)
Async XLA Ops:
  6.5 1.0 copy-start
  6.5 5.5 copy-start.2
  6.5 28.4 %reduce-scatter.13.cloned.1.call-start = ((), (), s32[]{:S(2)}) async-start(), calls=%async_computation.12 | async-start | bytes 327680 | tf_op jit(solution)/shard_map/reduce_scatter | solution.py:22
  12.0 117.8 %reduce-scatter.15.cloned.1.call-start = ((), (), s32[]{:S(2)}) async-start(), calls=%async_computation.13 | async-start | bytes 327680 | tf_op jit(solution)/shard_map/reduce_scatter | solution.py:22
  109.7 94.4 %reduce-scatter.25.cloned.1.call-start = ((), (), s32[]{:S(2)}) async-start(), calls=%async_computation.18 | async-start | bytes 589824
  223.8 13.1 %all-to-all-start.1 = ((bf16[8,2,8192]{2,1,0:T(2,128)(2,1)}), bf16[8,2,8192]{2,1,0:T(2,128)(2,1)S(1)}, u32[]{:S(2)}, u32[]{:S(2)}) async-start(bf16[8,2,8192]{2,1,0:T(2,128)(2,1)} %reshape.25), calls=%async_computation.3 | async-start | bytes 524288 | tf_op jit(solution)/shard_map/all_to_all | solution.py:47
  227.4 97.7 %reduce-scatter.17.cloned.1.call-start = ((), (), s32[]{:S(2)}) async-start(), calls=%async_computation.14 | async-start | bytes 589824 | tf_op jit(solution)/shard_map/reduce_scatter | solution.py:38
  262.9 151.1 %reduce-scatter.19.cloned.1.call-start = ((), (), s32[]{:S(2)}) async-start(), calls=%async_computation.15 | async-start | bytes 327680 | tf_op jit(solution)/shard_map/reduce_scatter | solution.py:22
  394.9 113.9 %reduce-scatter.21.cloned.1.call-start = ((), (), s32[]{:S(2)}) async-start(), calls=%async_computation.16 | async-start | bytes 327680 | tf_op jit(solution)/shard_map/reduce_scatter | solution.py:22
  488.6 94.6 %reduce-scatter.27.cloned.1.call-start = ((), (), s32[]{:S(2)}) async-start(), calls=%async_computation.19 | async-start | bytes 589824
  519.9 183.6 %reduce-scatter.23.cloned.1.call-start = ((), (), s32[]{:S(2)}) async-start(), calls=%async_computation.17 | async-start | bytes 589824 | tf_op jit(solution)/shard_map/reduce_scatter | solution.py:38
  637.5 132.5 %copy-start.1 = (bf16[2,64,2048]{2,1,0:T(8,128)(2,1)S(1)}, bf16[2,64,2048]{2,1,0:T(8,128)(2,1)}, u32[]{:S(2)}) copy-start(bf16[2,64,2048]{2,1,0:T(8,128)(2,1)} %param.8) | copy-start | bytes 1572868
Sparse Core Ops, SparseCore 0:
  12.1 22.7 reduce-scatter.12
  109.8 19.9 reduce-scatter.14
  141.0 63.0 reduce-scatter.24
  263.1 62.0 reduce-scatter.16
  395.0 18.9 reduce-scatter.18
  488.7 20.0 reduce-scatter.20
  520.1 63.1 reduce-scatter.26
  641.4 62.1 reduce-scatter.22
where the time goes:
time: 779 us; the launch traced here: 777 us
  waiting for transfers between devices  342 us (44%)
  blocking collectives  206 us (26%)
  local copies, waits for them, and re-layouts  114 us (15%)
  other arithmetic  62.1 us (8%)
  matrix products  34.7 us (4%)
  between operations  13.8 us (2%)
    unnamed x10, waiting for transfers between devices  127 us
    reduce_scatter x2, waiting for transfers between devices, on_device(): lax.psum_scatter(partial_in.astype(jnp.bfloat16), 'row', scatter_dimensio...  124 us
    reduce_scatter x4, waiting for transfers between devices, on_device(): lax.psum_scatter(partial_out.astype(jnp.bfloat16), 'col', scatter_dimensi...  82.1 us
    all_gather x2, blocking collectives, on_device(): image_panel = lax.all_gather(pieces, 'row', axis=2, tiled=True)  63.4 us
    all_gather x2, blocking collectives, on_device(): spread = lax.all_gather(scaled, 'row', axis=2, tiled=True)  63.1 us
    unnamed x24, local copies, waits for them, and re-layouts  49.6 us
    another operation x7, other arithmetic, on_device(): factor = jnp.linalg.cholesky(gram_sum / WIDTH)  23.8 us
    all_to_all x2, blocking collectives, on_device(): lax.all_to_all(spread, 'col', split_axis=2, concat_axis=1, tiled=True)  22.4 us
  transfers between devices with their start and end apart: 9, of which 9 were waited for; matrix products, arithmetic and copies ran while one was open for 0% of the time, Pallas kernels for 0%

commit v1 on v0

--- a/solution.py
+++ b/solution.py
@@ -24,7 +24,16 @@
             ).astype(jnp.float32)
             scaled = (slopes[:, layer_at, None, :] * summed).astype(jnp.bfloat16)
             if layer_at + 1 < layers:
-                spread = lax.all_gather(scaled, "row", axis=2, tiled=True)
+                ring = [scaled]
+                for hop in range(7):
+                    ring.append(
+                        lax.ppermute(ring[-1], "row", [(dev, (dev + 1) % 8) for dev in range(8)])
+                    )
+                spread = jnp.roll(
+                    jnp.concatenate(ring[::-1], axis=2),
+                    (lax.axis_index("row") + 1) * ring[0].shape[2],
+                    axis=2,
+                )
                 current = lax.all_to_all(spread, "col", split_axis=2, concat_axis=1, tiled=True)
             else:
                 cotangent = lax.all_gather(scaled, "col", axis=1, tiled=True)

time: 779 us -> 818 us (1.050)
  waiting for transfers between devices: 342 us -> 430 us
  blocking collectives: 206 us -> 142 us
    ppermute x0 -> x14, waiting for transfers between devices: none -> 95.6 us  [on_device(): lax.ppermute(ring[-1], 'row', [(dev, (dev + 1) % 8) for dev in range(8)])]
    all_gather x2 -> x0, blocking collectives: 63.1 us -> none  [on_device(): spread = lax.all_gather(scaled, 'row', axis=2, tiled=True)]
    dynamic_slice x0 -> x2, local copies, waits for them, and re-layouts: none -> 13.4 us  [on_device(): jnp.roll(jnp.concatenate(ring[::-1], axis=2), (lax.axis_index('row') + 1)...]
    all_gather x2 -> x0, local copies, waits for them, and re-layouts: 13.4 us -> none  [on_device(): spread = lax.all_gather(scaled, 'row', axis=2, tiled=True)]
    unnamed x24 -> x38, local copies, waits for them, and re-layouts: 49.6 us -> 49.7 us
  transfers between devices with their start and end apart: 9 -> 23, of which waited for: 9 -> 23; matrix products, arithmetic and copies ran while one was open for 0% -> 0% of each run, Pallas kernels for 0% -> 0%
where the time goes in v1:
time: 818 us; the launch traced here: 808 us
  waiting for transfers between devices  430 us (53%)
  blocking collectives  142 us (17%)
  local copies, waits for them, and re-layouts  115 us (14%)
  other arithmetic  64.8 us (8%)
  matrix products  34.7 us (4%)
  between operations  14.2 us (2%)
    unnamed x10, waiting for transfers between devices  127 us
    reduce_scatter x2, waiting for transfers between devices, on_device(): lax.psum_scatter(partial_in.astype(jnp.bfloat16), 'row', scatter_dimensio...  125 us
    ppermute x14, waiting for transfers between devices, on_device(): lax.ppermute(ring[-1], 'row', [(dev, (dev + 1) % 8) for dev in range(8)])  95.6 us
    reduce_scatter x4, waiting for transfers between devices, on_device(): lax.psum_scatter(partial_out.astype(jnp.bfloat16), 'col', scatter_dimensi...  74.7 us
    all_gather x2, blocking collectives, on_device(): image_panel = lax.all_gather(pieces, 'row', axis=2, tiled=True)  63.4 us
    unnamed x38, local copies, waits for them, and re-layouts  49.7 us
    another operation x7, other arithmetic, on_device(): factor = jnp.linalg.cholesky(gram_sum / WIDTH)  23.8 us
    all_to_all x2, blocking collectives, on_device(): lax.all_to_all(spread, 'col', split_axis=2, concat_axis=1, tiled=True)  22.4 us
  transfers between devices with their start and end apart: 23, of which 23 were waited for; matrix products, arithmetic and copies ran while one was open for 0% of the time, Pallas kernels for 0%

profile of v1, /device:TPU:0, one launch (start us, length us, event | category | flops | bytes accessed | tf_op | source)
XLA Modules:
  0.0 808.3 jit_solution(4975356674847637902)
XLA Ops:
  12.1 22.8 %reduce-scatter.13.cloned.1.call-done = bf16[2,16,1024]{2,1,0:T(8,128)(2,1)} async-done(((bf16[2,64,1024]{2,1,0:T(8,128)(2,1)}), bf16[2,16,1024]{2,1,0:T(8,128)(2,1)}) %reduce-scatter.13.cloned.1.call-update) | async-done | bytes 65552 | tf_op jit(solution)/shard_map/reduce_scatter | solution.py:22
  42.8 7.0 collective-permute-done.1
  49.8 7.0 collective-permute-done.2
  56.7 7.0 collective-permute-done.3
  63.7 7.5 collective-permute-done.4
  71.2 7.0 collective-permute-done.5
  99.1 11.2 %all_to_all.54 = bf16[4,2,32768]{2,1,0:T(2,128)(2,1)S(1)} all-to-all(bf16[4,2,32768]{2,1,0:T(2,128)(2,1)S(1)} %reshape.23), channel_id=1, replica_groups=mesh['row'=8,'col'=4] {'col'}, dimensions={0} | all-to-all | bytes 1048576 | tf_op jit(solution)/shard_map/all_to_all | solution.py:37
  114.4 9.7 %copy.67 = bf16[2,16,4,2048]{3,2,1,0:T(4,128)(2,1)S(1)} copy(bf16[2,16,4,2048]{1,0,3,2:T(2,128)(2,1)} %bitcast.105) | data formatting | bytes 1048576 | tf_op jit(solution)/shard_map/all_to_all | solution.py:37
  128.9 16.3 %reduce-scatter.15.cloned.1.call-done = bf16[2,16,1024]{2,1,0:T(8,128)(2,1)} async-done(((bf16[2,64,1024]{2,1,0:T(8,128)(2,1)}), bf16[2,16,1024]{2,1,0:T(8,128)(2,1)}) %reduce-scatter.15.cloned.1.call-update) | async-done | bytes 65552 | tf_op jit(solution)/shard_map/reduce_scatter | solution.py:22
  156.3 63.2 %reduce-scatter.25.cloned.1.call-done = bf16[8,4096]{1,0:T(8,128)(2,1)} async-done(((bf16[64,4096]{1,0:T(8,128)(2,1)}), bf16[8,4096]{1,0:T(8,128)(2,1)}) %reduce-scatter.25.cloned.1.call-update) | async-done | bytes 65552
  243.6 8.7 %all-to-all-done.1 = bf16[8,2,8192]{2,1,0:T(2,128)(2,1)S(1)} async-done(((bf16[8,2,8192]{2,1,0:T(2,128)(2,1)}), bf16[8,2,8192]{2,1,0:T(2,128)(2,1)S(1)}, u32[]{:S(2)}, u32[]{:S(2)}) %all-to-all-start.1) | async-done | bytes 262176 | tf_op jit(solution)/shard_map/all_to_all | solution.py:56
  258.3 7.5 fusion.2
  265.8 8.9 %copy.51 = bf16[2,8,8,1024]{3,2,1,0:T(8,128)(2,1)S(1)} copy(bf16[2,8,8,1024]{2,0,3,1:T(2,128)(2,1)} %fusion.2) | data formatting | bytes 524288 | tf_op jit(solution)/shard_map/convert_element_type | solution.py:42
  278.5 62.2 %reduce-scatter.17.cloned.1.call-done = bf16[2,64,256]{2,1,0:T(8,128)(2,1)} async-done(((bf16[2,64,2048]{2,1,0:T(8,128)(2,1)}), bf16[2,64,256]{2,1,0:T(8,128)(2,1)}) %reduce-scatter.17.cloned.1.call-update) | async-done | bytes 65552 | tf_op jit(solution)/shard_map/reduce_scatter | solution.py:47
  340.7 31.7 %all_gather.20 = bf16[2,64,2048]{2,1,0:T(8,128)(2,1)S(1)} all-gather(bf16[2,64,256]{2,1,0:T(8,128)(2,1)} %reduce-scatter.17.cloned.1.call-done), channel_id=1, replica_groups=mesh['row'=8,'col'=4] {'row'}, dimensions={2}, use_global_device_ids=true | all-gather | bytes 589824 | tf_op jit(solution)/shard_map/all_gather | solution.py:50
  372.7 10.3 %psum.14 = bf16[2,64,64]{1,2,0:T(8,128)(2,1)S(1)} all-reduce(bf16[2,64,64]{1,2,0:T(8,128)(2,1)S(1)} %convolution_convert_fusion.2), channel_id=1, replica_groups=mesh['row'=8,'col'=4] {'col'}, use_global_device_ids=true, to_apply=%region_4.6 | all-reduce | flops 8192 | bytes 32768 | tf_op jit(solution)/shard_map/psum | solution.py:60
  383.1 11.7 %custom-call.8 = f32[2,64,64]{2,1,0:T(8,128)S(1)} custom-call(f32[2,64,64]{2,1,0:T(8,128)S(1)} %fusion.64), custom_call_target="Cholesky" | custom-call | tf_op jit(solution)/shard_map/jit(cholesky)/cholesky | solution.py:61
  395.1 9.8 %custom-call.9 = f32[2,1,64,64]{2,3,1,0:T(8,128)S(1)} custom-call(f32[2,1,64,64]{3,2,1,0:T(8,128)S(1)} %select_bitcast_fusion.1), custom_call_target="InvertDiagBlocksLowerTriangular" | custom-call | tf_op jit(solution)/shard_map/vmap(jit(_solve_triangular))/triangular_solve | solution.py:62
  410.5 19.2 %reduce-scatter.19.cloned.1.call-done = bf16[2,16,1024]{2,1,0:T(8,128)(2,1)} async-done(((bf16[2,64,1024]{2,1,0:T(8,128)(2,1)}), bf16[2,16,1024]{2,1,0:T(8,128)(2,1)}) %reduce-scatter.19.cloned.1.call-update) | async-done | bytes 65552 | tf_op jit(solution)/shard_map/reduce_scatter | solution.py:22
  458.5 7.5 collective-permute-done.11
  494.0 11.2 %all_to_all.55 = bf16[4,2,32768]{2,1,0:T(2,128)(2,1)S(1)} all-to-all(bf16[4,2,32768]{2,1,0:T(2,128)(2,1)S(1)} %reshape.27), channel_id=1, replica_groups=mesh['row'=8,'col'=4] {'col'}, dimensions={0} | all-to-all | bytes 1048576 | tf_op jit(solution)/shard_map/all_to_all | solution.py:37
  509.4 9.7 %copy.68 = bf16[2,16,4,2048]{3,2,1,0:T(4,128)(2,1)S(1)} copy(bf16[2,16,4,2048]{1,0,3,2:T(2,128)(2,1)} %bitcast.107) | data formatting | bytes 1048576 | tf_op jit(solution)/shard_map/all_to_all | solution.py:37
  523.8 16.3 %reduce-scatter.21.cloned.1.call-done = bf16[2,16,1024]{2,1,0:T(8,128)(2,1)} async-done(((bf16[2,64,1024]{2,1,0:T(8,128)(2,1)}), bf16[2,16,1024]{2,1,0:T(8,128)(2,1)}) %reduce-scatter.21.cloned.1.call-update) | async-done | bytes 65552 | tf_op jit(solution)/shard_map/reduce_scatter | solution.py:22
  551.3 63.2 %reduce-scatter.27.cloned.1.call-done = bf16[8,4096]{1,0:T(8,128)(2,1)} async-done(((bf16[64,4096]{1,0:T(8,128)(2,1)}), bf16[8,4096]{1,0:T(8,128)(2,1)}) %reduce-scatter.27.cloned.1.call-update) | async-done | bytes 65552
  633.6 13.0 %all_to_all.56 = bf16[8,2,8192]{2,1,0:T(2,128)(2,1)S(1)} all-to-all(bf16[8,2,8192]{2,1,0:T(2,128)(2,1)S(1)} %reshape.29), channel_id=1, replica_groups=mesh['row'=8,'col'=4] {'row'}, dimensions={0} | all-to-all | bytes 524288 | tf_op jit(solution)/shard_map/all_to_all | solution.py:56
  652.6 7.5 fusion.3
  660.1 8.9 %copy.59 = bf16[2,8,8,1024]{3,2,1,0:T(8,128)(2,1)S(1)} copy(bf16[2,8,8,1024]{2,0,3,1:T(2,128)(2,1)} %fusion.3) | data formatting | bytes 524288 | tf_op jit(solution)/shard_map/convert_element_type | solution.py:42
  672.8 62.3 %reduce-scatter.23.cloned.1.call-done = bf16[2,64,256]{2,1,0:T(8,128)(2,1)} async-done(((bf16[2,64,2048]{2,1,0:T(8,128)(2,1)}), bf16[2,64,256]{2,1,0:T(8,128)(2,1)}) %reduce-scatter.23.cloned.1.call-update) | async-done | bytes 65552 | tf_op jit(solution)/shard_map/reduce_scatter | solution.py:47
  735.1 31.7 %all_gather.23 = bf16[2,64,2048]{2,1,0:T(8,128)(2,1)S(1)} all-gather(bf16[2,64,256]{2,1,0:T(8,128)(2,1)} %reduce-scatter.23.cloned.1.call-done), channel_id=1, replica_groups=mesh['row'=8,'col'=4] {'row'}, dimensions={2}, use_global_device_ids=true | all-gather | bytes 589824 | tf_op jit(solution)/shard_map/all_gather | solution.py:50
  767.0 10.3 %psum.15 = bf16[2,64,64]{1,2,0:T(8,128)(2,1)S(1)} all-reduce(bf16[2,64,64]{1,2,0:T(8,128)(2,1)S(1)} %convolution_convert_fusion.1), channel_id=1, replica_groups=mesh['row'=8,'col'=4] {'col'}, use_global_device_ids=true, to_apply=%region_11.15 | all-reduce | flops 8192 | bytes 32768 | tf_op jit(solution)/shard_map/psum | solution.py:60
  777.4 11.7 %custom-call.10 = f32[2,64,64]{2,1,0:T(8,128)S(1)} custom-call(f32[2,64,64]{2,1,0:T(8,128)S(1)} %fusion.62), custom_call_target="Cholesky" | custom-call | tf_op jit(solution)/shard_map/jit(cholesky)/cholesky | solution.py:61
  789.4 9.8 %custom-call.11 = f32[2,1,64,64]{2,3,1,0:T(8,128)S(1)} custom-call(f32[2,1,64,64]{3,2,1,0:T(8,128)S(1)} %select_bitcast_fusion), custom_call_target="InvertDiagBlocksLowerTriangular" | custom-call | tf_op jit(solution)/shard_map/vmap(jit(_solve_triangular))/triangular_solve | solution.py:62
  (124 shorter events, 202.3 us)
Async XLA Ops:
  6.5 1.0 copy-start
  6.5 5.5 copy-start.2
  6.5 28.4 %reduce-scatter.13.cloned.1.call-start = ((), (), s32[]{:S(2)}) async-start(), calls=%async_computation.12 | async-start | bytes 327680 | tf_op jit(solution)/shard_map/reduce_scatter | solution.py:22
  12.0 133.2 %reduce-scatter.15.cloned.1.call-start = ((), (), s32[]{:S(2)}) async-start(), calls=%async_computation.13 | async-start | bytes 327680 | tf_op jit(solution)/shard_map/reduce_scatter | solution.py:22
  35.8 7.0 collective-permute-start
  42.8 7.0 collective-permute-start.1
  49.8 7.0 collective-permute-start.2
  56.7 7.0 collective-permute-start.3
  63.7 7.5 collective-permute-start.4
  71.2 7.0 collective-permute-start.5
  78.2 7.0 collective-permute-start.6
  128.8 90.7 %reduce-scatter.25.cloned.1.call-start = ((), (), s32[]{:S(2)}) async-start(), calls=%async_computation.18 | async-start | bytes 589824
  239.3 13.1 %all-to-all-start.1 = ((bf16[8,2,8192]{2,1,0:T(2,128)(2,1)}), bf16[8,2,8192]{2,1,0:T(2,128)(2,1)S(1)}, u32[]{:S(2)}, u32[]{:S(2)}) async-start(bf16[8,2,8192]{2,1,0:T(2,128)(2,1)} %reshape.25), calls=%async_computation.3 | async-start | bytes 524288 | tf_op jit(solution)/shard_map/all_to_all | solution.py:56
  242.9 97.8 %reduce-scatter.17.cloned.1.call-start = ((), (), s32[]{:S(2)}) async-start(), calls=%async_computation.14 | async-start | bytes 589824 | tf_op jit(solution)/shard_map/reduce_scatter | solution.py:47
  278.4 151.4 %reduce-scatter.19.cloned.1.call-start = ((), (), s32[]{:S(2)}) async-start(), calls=%async_computation.15 | async-start | bytes 327680 | tf_op jit(solution)/shard_map/reduce_scatter | solution.py:22
  410.5 129.7 %reduce-scatter.21.cloned.1.call-start = ((), (), s32[]{:S(2)}) async-start(), calls=%async_computation.16 | async-start | bytes 327680 | tf_op jit(solution)/shard_map/reduce_scatter | solution.py:22
  430.6 7.0 collective-permute-start.7
  437.6 7.0 collective-permute-start.8
  444.6 7.0 collective-permute-start.9
  451.6 7.0 collective-permute-start.10
  458.5 7.5 collective-permute-start.11
  466.1 7.0 collective-permute-start.12
  473.0 7.1 collective-permute-start.13
  523.8 90.7 %reduce-scatter.27.cloned.1.call-start = ((), (), s32[]{:S(2)}) async-start(), calls=%async_computation.19 | async-start | bytes 589824
  551.3 183.8 %reduce-scatter.23.cloned.1.call-start = ((), (), s32[]{:S(2)}) async-start(), calls=%async_computation.17 | async-start | bytes 589824 | tf_op jit(solution)/shard_map/reduce_scatter | solution.py:47
  669.0 132.3 %copy-start.1 = (bf16[2,64,2048]{2,1,0:T(8,128)(2,1)S(1)}, bf16[2,64,2048]{2,1,0:T(8,128)(2,1)}, u32[]{:S(2)}) copy-start(bf16[2,64,2048]{2,1,0:T(8,128)(2,1)} %param.10) | copy-start | bytes 1572868
Sparse Core Ops, SparseCore 0:
  12.1 22.7 reduce-scatter.12
  129.0 16.2 reduce-scatter.14
  156.4 63.0 reduce-scatter.24
  278.5 62.1 reduce-scatter.16
  410.6 19.1 reduce-scatter.18
  523.9 16.2 reduce-scatter.20
  551.4 63.0 reduce-scatter.26
  672.9 62.1 reduce-scatter.22
